TPU v7x, 128 devices: a whole 4x4x4 slice. The times are simulated.
128 devices in a mesh: rows: 32 (over x, z, core), rel: 4 (over y).
Axes of the slice: x: 4, y: 4, z: 4, core: 2. Of those that a mesh axis runs over, the one named last changes fastest.
Arguments:
- features: bfloat16 [16384, 256], P('rows'), may hold values from -6 to 6
- bases: bfloat16 [8, 256, 256], replicated, may hold values from -0.125 to 0.125
- root: bfloat16 [256, 256], replicated, may hold values from -0.375 to 0.375
- coeffs: float32 [800, 8], P('rel'), may hold values from -4 to 4
- tiles: bfloat16 [32, 4, 64, 128, 128], P('rows', 'rel'), as said below
- tile_dst: int32 [32, 4, 64], P('rows', 'rel'), may hold values from 0 to 3
- tile_src: int32 [32, 4, 64], P('rows', 'rel'), may hold values from 0 to 63
- tile_rel: int32 [32, 4, 64], P('rows', 'rel'), may hold values from 0 to 199
- tile_live: int32 [32, 4], P('rows', 'rel'), may hold values from 16 to 64, as said below
- send_list: int32 [32, 4, 32, 2], P('rows', 'rel'), may hold values from 0 to 3
- cotangent: bfloat16 [16384, 256], P('rows'), may hold values from -6 to 6
Outputs:
- output: bfloat16 [16384, 256], P('rows')
- feature_grad: float32 [16384, 256], P('rows')
- basis_grad: float32 [8, 256, 256], replicated
- root_grad: float32 [256, 256], replicated
Inputs may be any that keep to these rules, and one draw needn't show every extreme that they name: `tile_live`: at least one device uses all 64 tile slots. `tiles`: entries are zero or positive, at most 12 / sqrt(2048).
All inputs are finite; a program needn't handle non-finite values.
Results may differ from a plain program's by a relative error of at most 0.0029.
Values may be sent and summed in bfloat16 or wider, within the bound.
A program may use at most 128 MiB of HBM per device.

v0:
```python
import math
import jax
import jax.numpy as jnp
from jax import lax
from jax.sharding import PartitionSpec as P


def on_device(
    features,
    bases,
    root,
    coeffs,
    tiles,
    tile_dst,
    tile_src,
    tile_rel,
    tile_live,
    send_list,
    cotangent,
):
    highest = lax.Precision.HIGHEST
    contract_first = (((0,), (0,)), ((), ()))
    feat_width = features.shape[1]
    size_block = tiles.shape[-1]
    blocks = features.reshape(-1, size_block, feat_width)
    local_blocks = blocks.shape[0]
    num_bases = bases.shape[0]
    slots_peer = send_list.shape[-1]
    row_devices = lax.axis_size("rows")
    total_slots = row_devices * slots_peer
    count_tiles = tiles.shape[2]
    adjacency = tiles[0, 0]
    dst_ids = tile_dst[0, 0]
    src_ids = tile_src[0, 0]
    rel_ids = tile_rel[0, 0]
    live_count = tile_live[0, 0]
    send_rows = send_list[0, 0]
    outgoing = blocks[send_rows]
    incoming = lax.all_to_all(outgoing, "rows", split_axis=0, concat_axis=0, tiled=True)
    received = incoming.reshape(total_slots, size_block, feat_width)
    step_tiles = math.gcd(count_tiles, 64)
    steps_live = (live_count + step_tiles - 1) // step_tiles

    def tile_weights(first_tile):
        position = first_tile + jnp.arange(step_tiles)
        in_use = (position < live_count).astype(jnp.float32)
        rel_hot = (rel_ids[:, None] == jnp.arange(coeffs.shape[0])[None, :]).astype(jnp.float32)
        coef_rows = jnp.dot(rel_hot, coeffs, precision=highest)
        dst_hot = (dst_ids[:, None] == jnp.arange(local_blocks)[None, :]).astype(
            jnp.float32
        ) * in_use[:, None]
        return (dst_hot[:, :, None] * coef_rows[:, None, :]).reshape(
            step_tiles, local_blocks * num_bases
        )

    def forward_step(block_index, running):
        first_tile = block_index * step_tiles
        sources = received[src_ids]
        messages = jnp.einsum(
            "tij,tjf->tif", adjacency, sources, preferred_element_type=jnp.float32
        )
        weights = tile_weights(first_tile)
        return running + lax.dot_general(
            weights, messages.reshape(step_tiles, -1), contract_first, precision=highest
        )

    zero_total = jnp.zeros((local_blocks * num_bases, size_block * feat_width), jnp.float32)
    partial_value = lax.fori_loop(0, steps_live, forward_step, zero_total)
    partial_value = partial_value.reshape(local_blocks, num_bases, size_block, feat_width)
    basis_f32 = bases.astype(jnp.float32)
    cot_blocks = cotangent.reshape(local_blocks, size_block, feat_width)
    cot_f32 = cot_blocks.astype(jnp.float32)
    root_term = jnp.dot(features, root, preferred_element_type=jnp.float32)
    rel_devices = lax.axis_size("rel")
    part_rows = features.shape[0] // rel_devices
    first_row = lax.axis_index("rel") * part_rows
    feat_part = lax.dynamic_slice_in_dim(features, first_row, part_rows)
    cot_part = lax.dynamic_slice_in_dim(cotangent, first_row, part_rows)
    root_local = lax.dot_general(
        feat_part, cot_part, contract_first, preferred_element_type=jnp.float32
    )
    projected_part = jnp.einsum("lbnf,bfg->lng", partial_value, basis_f32, precision=highest)
    basis_local = jnp.einsum("lbnf,lng->bfg", partial_value, cot_f32, precision=highest)
    projected = lax.psum(projected_part, "rel")
    basis_grad, root_grad = lax.psum((basis_local, root_local), ("rows", "rel"))
    output = (projected.reshape(-1, feat_width) + root_term).astype(jnp.bfloat16)
    agg_grad = jnp.einsum("lng,bfg->lbnf", cot_blocks, bases, preferred_element_type=jnp.float32)
    agg_grad = agg_grad.reshape(local_blocks * num_bases, size_block * feat_width)

    def backward_step(block_index, running):
        first_tile = block_index * step_tiles
        weights = tile_weights(first_tile)
        spread = jnp.dot(weights, agg_grad, precision=highest).astype(jnp.bfloat16)
        spread = spread.reshape(step_tiles, size_block, feat_width)
        backward_term = jnp.einsum(
            "tij,tif->tjf", adjacency, spread, preferred_element_type=jnp.float32
        )
        slot_hot = (src_ids[:, None] == jnp.arange(total_slots)[None, :]).astype(jnp.float32)
        return running + lax.dot_general(
            slot_hot, backward_term.reshape(step_tiles, -1), contract_first, precision=highest
        )

    slot_zero = jnp.zeros((total_slots, size_block * feat_width), jnp.float32)
    slot_grads = lax.fori_loop(0, steps_live, backward_step, slot_zero)
    returned = lax.all_to_all(
        slot_grads.reshape(row_devices, slots_peer, size_block * feat_width),
        "rows",
        split_axis=0,
        concat_axis=0,
        tiled=True,
    )
    block_hot = (send_rows.reshape(-1)[None, :] == jnp.arange(local_blocks)[:, None]).astype(
        jnp.float32
    )
    own_grads = jnp.dot(block_hot, returned.reshape(total_slots, -1), precision=highest)
    own_grads, projected = lax.optimization_barrier((own_grads, projected))
    summed = lax.psum(own_grads, "rel")
    root_back = lax.dot_general(
        cotangent, root, (((1,), (1,)), ((), ())), preferred_element_type=jnp.float32
    )
    feature_grad = summed.reshape(-1, feat_width) + root_back
    return (output, feature_grad, basis_grad, root_grad)


def solution(mesh):
    return jax.shard_map(
        on_device,
        mesh=mesh,
        in_specs=(
            P("rows", None),
            P(),
            P(),
            P("rel", None),
            P("rows", "rel", None, None, None),
            P("rows", "rel", None),
            P("rows", "rel", None),
            P("rows", "rel", None),
            P("rows", "rel"),
            P("rows", "rel", None, None),
            P("rows", None),
        ),
        out_specs=(P("rows", None), P("rows", None), P(), P()),
        check_vma=False,
    )
```

profile of v0, /device:TPU:1, one launch (start us, length us, event | category | flops | bytes accessed | tf_op | source)
XLA Modules:
  0.0 444.5 jit_solution(7627320191184519020)
XLA Ops:
  7.2 0.0 copy-start
  7.2 0.8 compare_select_fusion
  8.0 0.1 copy.24
  8.0 0.1 reshape.248
  8.2 3.7 gather_fusion
  11.9 9.6 %all-to-all-start = ((bf16[32,2,128,256]{3,2,1,0:T(8,128)(2,1)}), bf16[32,2,128,256]{3,2,1,0:T(8,128)(2,1)}, u32[]{:S(2)}, u32[]{:S(2)}) async-start(bf16[32,2,128,256]{3,2,1,0:T(8,128)(2,1)} %bitcast.121), calls=%async_computation | async-start | bytes 8388608 | tf_op jit(solution)/shard_map/all_to_all | solution.py:39
  22.1 0.0 copy-done
  22.2 0.0 copy-done.4
  22.2 2.7 convolution_bitcast_fusion.1
  24.8 5.5 %copy.36 = f32[4,8,128,256]{3,1,2,0:T(8,128)} copy(f32[4,8,128,256]{2,3,0,1:T(8,128)} %convolution_bitcast_fusion.1) | data formatting | bytes 8388608
  30.4 0.0 copy-done.12
  30.4 0.0 copy-done.13
  30.4 0.2 fusion.27
  30.6 4.0 broadcast_in_dim.5
  34.5 0.0 copy-done.9
  34.5 0.0 copy-done.10
  34.5 40.2 %while.25 = (s32[]{:T(128)}, f32[64,32768]{1,0:T(8,128)}, s32[]{:T(128)}, s32[1,1,64]{2,1,0:T(1,128)S(1)}, s32[1,1,64]{2,1,0:T(1,128)S(1)}, /*index=5*/s32[]{:T(...) while((s32[]{:T(128)}, f32[64,32768]{1,0:T(8,128)}, ...), condition=%wide.region_4.5_spmd, body=%wide.region_3.4_spmd.sunk | while | flops 2956991232 | bytes 73405568 | solution.py:104
  35.0 0.7 compare_convert_fusion.5
  35.7 8.6 %convolution_convert_fusion.2 = bf16[64,32768]{1,0:T(8,128)(2,1)S(1)} fusion(f32[32,32768]{1,0:T(8,128)} %get-tuple-element.440, f32[64,8]{0,1:T(8,128)S(1)} %get-tuple-element.439, f32[64,4]{0,1:T(4,128)S(1)} %fusion.72), kind=kOutput, calls=%fused_computation.11.clone.1 | convolution fusion | flops 807405568 | bytes 8391680 | tf_op jit(solution)/shard_map/while/body/dot_general | solution.py:93
  44.2 1.1 copy.51
  45.3 6.1 %convolution_bitcast_fusion.3 = f32[64,128,256]{1,2,0:T(8,128)} fusion(bf16[64,128,256]{2,1,0:T(8,128)(2,1)S(1)} %bitcast.115, bf16[64,128,128]{2,1,0:T(8,128)(2,1)} %get-tuple-element.441), kind=kOutput, calls=%fused_computation.12.clone.1 | convolution fusion | flops 536870912 | bytes 14680064 | tf_op jit(solution)/shard_map/while/body/tij,tif->tjf/dot_general | solution.py:95
  51.5 9.2 %copy.52 = f32[8,8,128,256]{3,1,2,0:T(8,128)} copy(f32[8,8,128,256]{2,3,1,0:T(8,128)} %bitcast.113) | data formatting | bytes 16777216 | tf_op jit(solution)/shard_map/while
  60.7 14.1 %convolution_add_fusion.7 = f32[64,32768]{1,0:T(8,128)} fusion(f32[64,32768]{1,0:T(8,128)} %get-tuple-element.423, f32[64,32768]{1,0:T(8,128)} %bitcast.112, s32[64]{0:T(128)S(1)} %bitcast.127), kind=kOutput, calls=%fused_computation.10.clone.1 | convolution fusion | flops 1612713984 | bytes 25166080 | tf_op jit(solution)/shard_map/while/body/dot_general | solution.py:99
  74.8 10.6 %reshape.243 = f32[32,2,32768]{2,1,0:T(2,128)} reshape(f32[64,32768]{1,0:T(8,128)} %get-tuple-element.237) | data formatting | bytes 16777216 | tf_op jit(solution)/shard_map/reshape | solution.py:106
  85.4 0.0 all-to-all-done
  85.4 7.4 %all-to-all-start.1 = ((f32[32,2,32768]{2,1,0:T(2,128)}), f32[32,2,32768]{2,1,0:T(2,128)}, u32[]{:S(2)}, u32[]{:S(2)}) async-start(f32[32,2,32768]{2,1,0:T(2,128)} %reshape.243), calls=%async_computation.1 | async-start | bytes 16777216 | tf_op jit(solution)/shard_map/all_to_all | solution.py:105
  92.9 0.0 all-reduce.5.cloned.1.call-start
  92.9 4.9 %gather_fusion.1 = bf16[64,128,256]{2,1,0:T(8,128)(2,1)} fusion(bf16[64,128,256]{2,1,0:T(8,128)(2,1)} %bitcast.12, s32[1024]{0:T(1024)S(1)} %pad_clamp_fusion), kind=kCustom, calls=%fused_computation.1 | custom fusion | bytes 8388864 | tf_op jit(solution)/shard_map/while/body/gather | solution.py:58
  97.9 2.3 broadcast_in_dim.4
  100.1 18.3 %while.24 = (s32[]{:T(128)}, f32[32,32768]{1,0:T(8,128)}, s32[]{:T(128)}, s32[1,1,64]{2,1,0:T(1,128)S(1)}, s32[]{:T(128)}, /*index=5*/f32[64,8]{0,1:T(8,128)S(1)...) while((s32[]{:T(128)}, f32[32,32768]{1,0:T(8,128)}, s32[]{:T(128)}, ...), condition=%wide.region_1.2_spmd, body=%wide.region_0.1_spmd.sunk | while | flops 1343228672 | bytes 81793968 | solution.py:68
  100.1 0.6 compare_convert_fusion.4
  100.8 4.1 fusion.65
  104.9 0.0 copy-start.1
  104.9 4.7 %copy.50 = f32[8,8,128,256]{3,1,2,0:T(8,128)S(1)} copy(f32[8,8,128,256]{3,2,1,0:T(8,128)S(1)} %bitcast.114) | data formatting | bytes 16777216 | tf_op jit(solution)/shard_map/while
  109.6 0.0 copy-done.1
  109.6 6.6 %convolution_add_fusion.6 = f32[32,32768]{1,0:T(8,128)S(1)} fusion(f32[32,32768]{1,0:T(8,128)S(1)} %copy-done.1, f32[64,32768]{1,0:T(8,128)S(1)} %bitcast.111, f32[64,8]{0,1:T(8,128)S(1)} %get-tuple-element.406, f32[64,4]{0,1:T(4,128)S(1)} %fusion.66), kind=kOutput, calls=%fused_computation.2.clone.1 | convolution fusion | flops 806356992 | bytes 16780288 | tf_op jit(solution)/shard_map/while/body/dot_general | solution.py:63
  116.3 0.0 copy-start.2
  116.3 2.0 copy-done.2
  118.4 0.0 copy-start.11
  118.4 6.0 %fusion.18 = f32[4,128,256]{2,1,0:T(8,128)} fusion(f32[4,8,128,256]{3,1,2,0:T(8,128)} %bitcast.117, bf16[8,256,256]{2,1,0:T(8,128)(2,1)S(1)} %copy-done), kind=kOutput, calls=%fused_computation.28 | convolution fusion | flops 3221225472 | bytes 5767168 | tf_op jit(solution)/shard_map/lbnf,bfg->lng/dot_general | solution.py:82
  124.4 0.0 all-reduce.5.cloned.1.call-update
  124.4 0.0 all-reduce.7.cloned.1.call-start
  124.5 0.1 copy.26
  124.6 0.1 eq.116
  124.7 75.4 %all-to-all-done.1 = f32[32,2,32768]{2,1,0:T(2,128)} async-done(((f32[32,2,32768]{2,1,0:T(2,128)}), f32[32,2,32768]{2,1,0:T(2,128)}, u32[]{:S(2)}, u32[]{:S(2)}) %all-to-all-start.1) | async-done | bytes 8388640 | tf_op jit(solution)/shard_map/all_to_all | solution.py:105
  200.1 10.9 %reshape.244 = f32[64,32768]{1,0:T(8,128)} reshape(f32[32,2,32768]{2,1,0:T(2,128)} %all-to-all-done.1) | data formatting | bytes 16777216 | tf_op jit(solution)/shard_map/reshape | solution.py:115
  211.0 6.2 %fusion.29 = f32[4,32768]{1,0:T(4,128)S(1)} fusion(f32[64,32768]{1,0:T(8,128)} %reshape.244, s32[64]{0:T(128)S(1)} %eq.116), kind=kOutput, calls=%fused_computation.45 | convolution fusion | flops 100663552 | bytes 8913152 | tf_op jit(solution)/shard_map/dot_general | solution.py:115
  217.2 0.0 all-reduce.5.cloned.1.call-done
  217.2 1.2 reshape.245
  218.4 0.0 all-reduce.7.cloned.1.call-update
  218.4 0.3 all-reduce.9.cloned.1.call-start
  218.7 0.0 copy-done.3
  218.7 0.0 copy-done.5
  218.7 0.9 fusion.24
  219.6 7.6 %fusion.15 = f32[8,256,256]{2,1,0:T(8,128)} fusion(bf16[4,128,256,1]{2,1,0,3:T(8,128)(2,1)S(1)} %bitcast.123, f32[4,8,128,256]{3,1,2,0:T(8,128)} %bitcast.118), kind=kOutput, calls=%fused_computation.27 | convolution fusion | flops 3221225472 | bytes 6553600 | tf_op jit(solution)/shard_map/lbnf,lng->bfg/dot_general | solution.py:83
  227.3 0.0 all-reduce.9.cloned.1.call-update
  227.3 0.0 copy-done.6
  227.3 0.0 copy-done.7
  227.3 0.9 fusion.21
  228.2 45.5 %all-reduce.7.cloned.1.call-done = f32[512,256]{1,0:T(8,128)} async-done(((f32[512,256]{1,0:T(8,128)}), f32[512,256]{1,0:T(8,128)}) %all-reduce.7.cloned.1.call-update) | async-done | bytes 524304 | tf_op jit(solution)/shard_map/psum | solution.py:117
  273.7 2.1 convolution_add_fusion.2
  275.8 158.1 %all-reduce.9.cloned.1.call-done = (f32[8,256,256]{2,1,0:T(8,128)}, f32[256,256]{1,0:T(8,128)}) async-done(((f32[8,256,256]{2,1,0:T(8,128)}, f32[256,256]{1,0:T(8,128)}), (f32[8,256,256]{2,1,0:T(8,128)}, f32[256,256]{1,0:T(8,128)})) %all-reduce.9.cloned.1.call-update) | async-done | bytes 2359312 | tf_op jit(solution)/shard_map/psum | solution.py:85
  433.9 3.1 copy.70
  437.0 0.7 copy.71
  (17 shorter events, 0.0 us)
Async XLA Ops:
  7.2 15.0 %copy-start = (bf16[8,256,256]{2,1,0:T(8,128)(2,1)S(1)}, bf16[8,256,256]{2,1,0:T(8,128)(2,1)}, u32[]{:S(2)}) copy-start(bf16[8,256,256]{2,1,0:T(8,128)(2,1)} %param.16) | copy-start | bytes 3145732
  11.9 10.3 %copy-start.4 = (bf16[512,256]{1,0:T(8,128)(2,1)S(1)}, bf16[512,256]{1,0:T(8,128)(2,1)}, u32[]{:S(2)}) copy-start(bf16[512,256]{1,0:T(8,128)(2,1)} %param.25) | copy-start | bytes 786436
  11.9 73.5 %all-to-all-start = ((bf16[32,2,128,256]{3,2,1,0:T(8,128)(2,1)}), bf16[32,2,128,256]{3,2,1,0:T(8,128)(2,1)}, u32[]{:S(2)}, u32[]{:S(2)}) async-start(bf16[32,2,128,256]{3,2,1,0:T(8,128)(2,1)} %bitcast.121), calls=%async_computation | async-start | bytes 8388608 | tf_op jit(solution)/shard_map/all_to_all | solution.py:39
  24.8 5.5 %copy-start.12 = (f32[200,8]{0,1:T(8,128)S(1)}, f32[200,8]{0,1:T(8,128)}, u32[]{:S(2)}) copy-start(f32[200,8]{0,1:T(8,128)} %param.18) | copy-start | bytes 19204
  24.8 5.5 %copy-start.13 = (s32[1,1,64]{2,1,0:T(1,128)S(1)}, s32[1,1,64]{2,1,0:T(1,128)}, u32[]{:S(2)}) copy-start(s32[1,1,64]{2,1,0:T(1,128)} %param.22) | copy-start | bytes 772
  30.6 4.0 copy-start.9
  30.6 4.0 copy-start.10
  85.4 114.7 %all-to-all-start.1 = ((f32[32,2,32768]{2,1,0:T(2,128)}), f32[32,2,32768]{2,1,0:T(2,128)}, u32[]{:S(2)}, u32[]{:S(2)}) async-start(f32[32,2,32768]{2,1,0:T(2,128)} %reshape.243), calls=%async_computation.1 | async-start | bytes 16777216 | tf_op jit(solution)/shard_map/all_to_all | solution.py:105
  92.9 124.4 %all-reduce.5.cloned.1.call-start = ((), (), s32[]{:S(2)}) async-start(), calls=%async_computation.2 | async-start | bytes 1048576 | tf_op jit(solution)/shard_map/psum | solution.py:84
  104.9 4.8 %copy-start.1 = (f32[32,32768]{1,0:T(8,128)S(1)}, f32[32,32768]{1,0:T(8,128)}, u32[]{:S(2)}) copy-start(f32[32,32768]{1,0:T(8,128)} %get-tuple-element.392) | copy-start | bytes 12582916 | tf_op jit(solution)/shard_map/while
  116.3 2.0 copy-start.2
  118.4 6.1 %copy-start.11 = (s32[1,1,32,2]{2,3,1,0:T(2,128)S(1)}, s32[1,1,32,2]{2,3,1,0:T(2,128)}, u32[]{:S(2)}) copy-start(s32[1,1,32,2]{2,3,1,0:T(2,128)} %param.24) | copy-start | bytes 772
  124.4 149.3 %all-reduce.7.cloned.1.call-start = ((), (), s32[]{:S(2)}) async-start(), calls=%async_computation.3 | async-start | bytes 1048576 | tf_op jit(solution)/shard_map/psum | solution.py:117
  211.0 7.7 %copy-start.3 = (bf16[512,256]{1,0:T(8,128)(2,1)S(1)}, bf16[512,256]{1,0:T(8,128)(2,1)}, u32[]{:S(2)}) copy-start(bf16[512,256]{1,0:T(8,128)(2,1)} %param.15) | copy-start | bytes 786436
  211.0 7.7 %copy-start.5 = (bf16[512,256]{1,0:T(8,128)(2,1)S(1)}, bf16[512,256]{1,0:T(8,128)(2,1)}, u32[]{:S(2)}) copy-start(bf16[512,256]{1,0:T(8,128)(2,1)} %param.25) | copy-start | bytes 786436
  218.4 215.5 %all-reduce.9.cloned.1.call-start = ((), (), s32[]{:S(2)}) async-start(), calls=%async_computation.4 | async-start | bytes 4718592 | tf_op jit(solution)/shard_map/psum | solution.py:85
  219.6 7.7 %copy-start.6 = (f32[4,128,256]{2,1,0:T(8,128)S(1)}, f32[4,128,256]{2,1,0:T(8,128)}, u32[]{:S(2)}) copy-start(f32[4,128,256]{2,1,0:T(8,128)} %all-reduce.5.cloned.1.call-done) | copy-start | bytes 1572868
  219.6 7.7 %copy-start.7 = (bf16[256,256]{1,0:T(8,128)(2,1)S(1)}, bf16[256,256]{1,0:T(8,128)(2,1)}, u32[]{:S(2)}) copy-start(bf16[256,256]{1,0:T(8,128)(2,1)} %param.17) | copy-start | bytes 393220
  433.9 3.1 copy-start.8
Sparse Core Ops, SparseCore 0:
  124.6 42.8 all-reduce.4
  218.5 55.1 all-reduce.6
  279.2 154.6 all-reduce.8
where the time goes:
time: 448 us; the launch traced here: 444 us
  waiting for transfers between devices  279 us (62%)
  matrix products  66.1 us (15%)
  local copies, waits for them, and re-layouts  64.4 us (14%)
  starting transfers between devices  17.4 us (4%)
  between operations  14.8 us (3%)
    psum x1, waiting for transfers between devices, on_device(): basis_grad, root_grad = lax.psum((basis_local, root_local), ('rows', 'rel'))  158 us
    all_to_all x1, waiting for transfers between devices, on_device(): lax.all_to_all(slot_grads.reshape(row_devices, slots_peer, size_block * f...  75.4 us
    psum x1, waiting for transfers between devices, on_device(): summed = lax.psum(own_grads, 'rel')  45.5 us
    while x7, local copies, waits for them, and re-layouts  17 us
    dot_general x1, matrix products, backward_step(): lax.dot_general(slot_hot, backward_term.reshape(step_tiles, -1), contract...  14.1 us
    reshape x1, local copies, waits for them, and re-layouts, on_device(): returned.reshape(total_slots, -1)  10.9 us
    reshape x1, local copies, waits for them, and re-layouts, on_device(): slot_grads.reshape(row_devices, slots_peer, size_block * feat_width)  10.6 us
    all_to_all x1, starting transfers between devices, on_device(): lax.all_to_all(outgoing, 'rows', split_axis=0, concat_axis=0, tiled=True)  9.61 us
  transfers between devices with their start and end apart: 5, of which 3 were waited for; matrix products, arithmetic and copies ran while one was open for 27% of the time, Pallas kernels for 0%

commit v1 on v0

--- a/solution.py
+++ b/solution.py
@@ -3,6 +3,7 @@
 import jax.numpy as jnp
 from jax import lax
 from jax.sharding import PartitionSpec as P
+from jax.lax import all_gather
 
 
 def on_device(
@@ -114,7 +115,7 @@
     )
     own_grads = jnp.dot(block_hot, returned.reshape(total_slots, -1), precision=highest)
     own_grads, projected = lax.optimization_barrier((own_grads, projected))
-    summed = lax.psum(own_grads, "rel")
+    summed = jnp.sum(all_gather(own_grads, "rel"), axis=0)
     root_back = lax.dot_general(
         cotangent, root, (((1,), (1,)), ((), ())), preferred_element_type=jnp.float32
     )

time: 448 us -> 414 us (0.924)
  waiting for transfers between devices: 279 us -> 243 us
    psum x1 -> x0, waiting for transfers between devices: 45.5 us -> none  [on_device(): summed = lax.psum(own_grads, 'rel')]
    all_gather x0 -> x1, waiting for transfers between devices: none -> 36.5 us  [on_device(): summed = jnp.sum(all_gather(own_grads, 'rel'), axis=0)]
    psum x1, waiting for transfers between devices: 158 us -> 131 us  [on_device(): basis_grad, root_grad = lax.psum((basis_local, root_local), ('rows', 'rel'))]
  transfers between devices with their start and end apart: 5 -> 5, of which waited for: 3 -> 3; matrix products, arithmetic and copies ran while one was open for 27% -> 30% of each run, Pallas kernels for 0% -> 0%
where the time goes in v1:
time: 414 us; the launch traced here: 411 us
  waiting for transfers between devices  243 us (59%)
  matrix products  65.9 us (16%)
  local copies, waits for them, and re-layouts  63.6 us (15%)
  starting transfers between devices  17.4 us (4%)
  between operations  16.5 us (4%)
  other arithmetic  4.19 us (1%)
    psum x1, waiting for transfers between devices, on_device(): basis_grad, root_grad = lax.psum((basis_local, root_local), ('rows', 'rel'))  131 us
    all_to_all x1, waiting for transfers between devices, on_device(): lax.all_to_all(slot_grads.reshape(row_devices, slots_peer, size_block * f...  75.4 us
    all_gather x1, waiting for transfers between devices, on_device(): summed = jnp.sum(all_gather(own_grads, 'rel'), axis=0)  36.5 us
    while x7, local copies, waits for them, and re-layouts  17 us
    dot_general x1, matrix products, backward_step(): lax.dot_general(slot_hot, backward_term.reshape(step_tiles, -1), contract...  14.1 us
    reshape x1, local copies, waits for them, and re-layouts, on_device(): returned.reshape(total_slots, -1)  10.9 us
    reshape x1, local copies, waits for them, and re-layouts, on_device(): slot_grads.reshape(row_devices, slots_peer, size_block * feat_width)  10.6 us
    all_to_all x1, starting transfers between devices, on_device(): lax.all_to_all(outgoing, 'rows', split_axis=0, concat_axis=0, tiled=True)  9.61 us
  transfers between devices with their start and end apart: 5, of which 3 were waited for; matrix products, arithmetic and copies ran while one was open for 30% of the time, Pallas kernels for 0%

profile of v1, /device:TPU:1, one launch (start us, length us, event | category | flops | bytes accessed | tf_op | source)
XLA Modules:
  0.0 410.8 jit_solution(710790758381918305)
XLA Ops:
  8.0 0.0 copy-start
  8.0 0.8 compare_select_fusion
  8.8 0.1 copy.31
  8.9 0.1 reshape.248
  9.0 3.7 gather_fusion
  12.7 9.6 %all-to-all-start = ((bf16[32,2,128,256]{3,2,1,0:T(8,128)(2,1)}), bf16[32,2,128,256]{3,2,1,0:T(8,128)(2,1)}, u32[]{:S(2)}, u32[]{:S(2)}) async-start(bf16[32,2,128,256]{3,2,1,0:T(8,128)(2,1)} %bitcast.122), calls=%async_computation | async-start | bytes 8388608 | tf_op jit(solution)/shard_map/all_to_all | solution.py:40
  23.0 0.0 copy-done
  23.0 0.0 copy-done.4
  23.0 2.7 convolution_bitcast_fusion.1
  25.7 5.5 %copy.43 = f32[4,8,128,256]{3,1,2,0:T(8,128)} copy(f32[4,8,128,256]{2,3,0,1:T(8,128)} %convolution_bitcast_fusion.1) | data formatting | bytes 8388608
  31.2 0.0 copy-done.12
  31.2 0.0 copy-done.13
  31.2 0.2 fusion.27
  31.4 4.0 broadcast_in_dim.5
  35.4 0.0 copy-done.9
  35.4 0.0 copy-done.10
  35.4 40.2 %while.25 = (s32[]{:T(128)}, f32[64,32768]{1,0:T(8,128)}, s32[]{:T(128)}, s32[1,1,64]{2,1,0:T(1,128)S(1)}, s32[1,1,64]{2,1,0:T(1,128)S(1)}, /*index=5*/s32[]{:T(...) while((s32[]{:T(128)}, f32[64,32768]{1,0:T(8,128)}, ...), condition=%wide.region_4.5_spmd, body=%wide.region_3.4_spmd.sunk | while | flops 2956991232 | bytes 73405568 | solution.py:105
  35.8 0.7 compare_convert_fusion.5
  36.5 8.6 %convolution_convert_fusion.2 = bf16[64,32768]{1,0:T(8,128)(2,1)S(1)} fusion(f32[32,32768]{1,0:T(8,128)} %get-tuple-element.440, f32[64,8]{0,1:T(8,128)S(1)} %get-tuple-element.439, f32[64,4]{0,1:T(4,128)S(1)} %fusion.72), kind=kOutput, calls=%fused_computation.11.clone.1 | convolution fusion | flops 807405568 | bytes 8391680 | tf_op jit(solution)/shard_map/while/body/dot_general | solution.py:94
  45.1 1.1 copy.58
  46.2 6.1 %convolution_bitcast_fusion.3 = f32[64,128,256]{1,2,0:T(8,128)} fusion(bf16[64,128,256]{2,1,0:T(8,128)(2,1)S(1)} %bitcast.116, bf16[64,128,128]{2,1,0:T(8,128)(2,1)} %get-tuple-element.441), kind=kOutput, calls=%fused_computation.12.clone.1 | convolution fusion | flops 536870912 | bytes 14680064 | tf_op jit(solution)/shard_map/while/body/tij,tif->tjf/dot_general | solution.py:96
  52.3 9.2 %copy.59 = f32[8,8,128,256]{3,1,2,0:T(8,128)} copy(f32[8,8,128,256]{2,3,1,0:T(8,128)} %bitcast.114) | data formatting | bytes 16777216 | tf_op jit(solution)/shard_map/while
  61.5 14.1 %convolution_add_fusion.7 = f32[64,32768]{1,0:T(8,128)} fusion(f32[64,32768]{1,0:T(8,128)} %get-tuple-element.423, f32[64,32768]{1,0:T(8,128)} %bitcast.113, s32[64]{0:T(128)S(1)} %bitcast.129), kind=kOutput, calls=%fused_computation.10.clone.1 | convolution fusion | flops 1612713984 | bytes 25166080 | tf_op jit(solution)/shard_map/while/body/dot_general | solution.py:100
  75.6 10.6 %reshape.243 = f32[32,2,32768]{2,1,0:T(2,128)} reshape(f32[64,32768]{1,0:T(8,128)} %get-tuple-element.237) | data formatting | bytes 16777216 | tf_op jit(solution)/shard_map/reshape | solution.py:107
  86.2 0.0 all-to-all-done
  86.2 7.4 %all-to-all-start.1 = ((f32[32,2,32768]{2,1,0:T(2,128)}), f32[32,2,32768]{2,1,0:T(2,128)}, u32[]{:S(2)}, u32[]{:S(2)}) async-start(f32[32,2,32768]{2,1,0:T(2,128)} %reshape.243), calls=%async_computation.1 | async-start | bytes 16777216 | tf_op jit(solution)/shard_map/all_to_all | solution.py:106
  93.7 0.0 all-reduce.4.cloned.1.call-start
  93.7 4.9 %gather_fusion.1 = bf16[64,128,256]{2,1,0:T(8,128)(2,1)} fusion(bf16[64,128,256]{2,1,0:T(8,128)(2,1)} %bitcast.12, s32[1024]{0:T(1024)S(1)} %pad_clamp_fusion), kind=kCustom, calls=%fused_computation.1 | custom fusion | bytes 8388864 | tf_op jit(solution)/shard_map/while/body/gather | solution.py:59
  98.7 2.3 broadcast_in_dim.4
  101.0 18.3 %while.24 = (s32[]{:T(128)}, f32[32,32768]{1,0:T(8,128)}, s32[]{:T(128)}, s32[1,1,64]{2,1,0:T(1,128)S(1)}, s32[]{:T(128)}, /*index=5*/f32[64,8]{0,1:T(8,128)S(1)...) while((s32[]{:T(128)}, f32[32,32768]{1,0:T(8,128)}, s32[]{:T(128)}, ...), condition=%wide.region_1.2_spmd, body=%wide.region_0.1_spmd.sunk | while | flops 1343228672 | bytes 81793968 | solution.py:69
  101.0 0.6 compare_convert_fusion.4
  101.6 4.1 fusion.65
  105.7 0.0 copy-start.1
  105.7 4.7 %copy.57 = f32[8,8,128,256]{3,1,2,0:T(8,128)S(1)} copy(f32[8,8,128,256]{3,2,1,0:T(8,128)S(1)} %bitcast.115) | data formatting | bytes 16777216 | tf_op jit(solution)/shard_map/while
  110.4 0.0 copy-done.1
  110.5 6.6 %convolution_add_fusion.6 = f32[32,32768]{1,0:T(8,128)S(1)} fusion(f32[32,32768]{1,0:T(8,128)S(1)} %copy-done.1, f32[64,32768]{1,0:T(8,128)S(1)} %bitcast.112, f32[64,8]{0,1:T(8,128)S(1)} %get-tuple-element.406, f32[64,4]{0,1:T(4,128)S(1)} %fusion.66), kind=kOutput, calls=%fused_computation.2.clone.1 | convolution fusion | flops 806356992 | bytes 16780288 | tf_op jit(solution)/shard_map/while/body/dot_general | solution.py:64
  117.1 0.0 copy-start.2
  117.1 2.0 copy-done.2
  119.2 0.0 copy-start.11
  119.3 6.0 %fusion.18 = f32[4,128,256]{2,1,0:T(8,128)} fusion(f32[4,8,128,256]{3,1,2,0:T(8,128)} %bitcast.118, bf16[8,256,256]{2,1,0:T(8,128)(2,1)S(1)} %copy-done), kind=kOutput, calls=%fused_computation.28 | convolution fusion | flops 3221225472 | bytes 5767168 | tf_op jit(solution)/shard_map/lbnf,bfg->lng/dot_general | solution.py:83
  125.2 0.0 all-reduce.4.cloned.1.call-update
  125.3 0.0 all-gather.4.cloned.1.call-start
  125.3 0.0 copy-done.11
  125.3 0.1 copy.33
  125.4 0.1 eq.116
  125.5 75.4 %all-to-all-done.1 = f32[32,2,32768]{2,1,0:T(2,128)} async-done(((f32[32,2,32768]{2,1,0:T(2,128)}), f32[32,2,32768]{2,1,0:T(2,128)}, u32[]{:S(2)}, u32[]{:S(2)}) %all-to-all-start.1) | async-done | bytes 8388640 | tf_op jit(solution)/shard_map/all_to_all | solution.py:106
  200.9 10.9 %reshape.244 = f32[64,32768]{1,0:T(8,128)} reshape(f32[32,2,32768]{2,1,0:T(2,128)} %all-to-all-done.1) | data formatting | bytes 16777216 | tf_op jit(solution)/shard_map/reshape | solution.py:116
  211.8 7.0 %fusion.29 = f32[4,32768]{1,0:T(4,128)} fusion(f32[64,32768]{1,0:T(8,128)} %reshape.244, s32[64]{0:T(128)S(1)} %eq.116), kind=kOutput, calls=%fused_computation.45 | convolution fusion | flops 100663552 | bytes 8913152 | tf_op jit(solution)/shard_map/dot_general | solution.py:116
  218.8 0.0 all-gather.4.cloned.1.call-update
  218.9 0.3 all-reduce.6.cloned.1.call-start
  219.1 0.0 copy-done.3
  219.1 0.0 copy-done.5
  219.2 0.9 fusion.24
  220.1 7.6 %fusion.15 = f32[8,256,256]{2,1,0:T(8,128)} fusion(bf16[4,128,256,1]{2,1,0,3:T(8,128)(2,1)S(1)} %bitcast.124, f32[4,8,128,256]{3,1,2,0:T(8,128)} %bitcast.119), kind=kOutput, calls=%fused_computation.27 | convolution fusion | flops 3221225472 | bytes 6553600 | tf_op jit(solution)/shard_map/lbnf,lng->bfg/dot_general | solution.py:84
  227.7 0.0 all-reduce.6.cloned.1.call-update
  227.7 0.9 fusion.21
  228.7 36.5 %all-gather.4.cloned.1.call-done = f32[4,4,32768]{2,1,0:T(4,128)} async-done(((f32[1,4,32768]{2,1,0:T(4,128)}), f32[4,4,32768]{2,1,0:T(4,128)}) %all-gather.4.cloned.1.call-update) | async-done | bytes 2097168 | tf_op jit(solution)/shard_map/all_gather | solution.py:118
  265.1 2.1 reduce_sum.9
  267.2 0.4 reshape.245
  267.6 1.1 convolution_add_fusion.2
  268.7 130.7 %all-reduce.6.cloned.1.call-done = (f32[8,256,256]{2,1,0:T(8,128)}, f32[256,256]{1,0:T(8,128)}) async-done(((f32[8,256,256]{2,1,0:T(8,128)}, f32[256,256]{1,0:T(8,128)}), (f32[8,256,256]{2,1,0:T(8,128)}, f32[256,256]{1,0:T(8,128)})) %all-reduce.6.cloned.1.call-update) | async-done | bytes 2359312 | tf_op jit(solution)/shard_map/psum | solution.py:86
  399.4 3.1 copy.76
  402.5 0.0 copy-done.8
  402.5 0.7 copy.77
  (18 shorter events, 0.0 us)
Async XLA Ops:
  8.0 15.0 %copy-start = (bf16[8,256,256]{2,1,0:T(8,128)(2,1)S(1)}, bf16[8,256,256]{2,1,0:T(8,128)(2,1)}, u32[]{:S(2)}) copy-start(bf16[8,256,256]{2,1,0:T(8,128)(2,1)} %param.16) | copy-start | bytes 3145732
  12.7 10.3 %copy-start.4 = (bf16[512,256]{1,0:T(8,128)(2,1)S(1)}, bf16[512,256]{1,0:T(8,128)(2,1)}, u32[]{:S(2)}) copy-start(bf16[512,256]{1,0:T(8,128)(2,1)} %param.25) | copy-start | bytes 786436
  12.7 73.5 %all-to-all-start = ((bf16[32,2,128,256]{3,2,1,0:T(8,128)(2,1)}), bf16[32,2,128,256]{3,2,1,0:T(8,128)(2,1)}, u32[]{:S(2)}, u32[]{:S(2)}) async-start(bf16[32,2,128,256]{3,2,1,0:T(8,128)(2,1)} %bitcast.122), calls=%async_computation | async-start | bytes 8388608 | tf_op jit(solution)/shard_map/all_to_all | solution.py:40
  25.7 5.5 %copy-start.12 = (f32[200,8]{0,1:T(8,128)S(1)}, f32[200,8]{0,1:T(8,128)}, u32[]{:S(2)}) copy-start(f32[200,8]{0,1:T(8,128)} %param.18) | copy-start | bytes 19204
  25.7 5.5 %copy-start.13 = (s32[1,1,64]{2,1,0:T(1,128)S(1)}, s32[1,1,64]{2,1,0:T(1,128)}, u32[]{:S(2)}) copy-start(s32[1,1,64]{2,1,0:T(1,128)} %param.22) | copy-start | bytes 772
  31.4 4.0 copy-start.9
  31.4 4.0 copy-start.10
  86.2 114.6 %all-to-all-start.1 = ((f32[32,2,32768]{2,1,0:T(2,128)}), f32[32,2,32768]{2,1,0:T(2,128)}, u32[]{:S(2)}, u32[]{:S(2)}) async-start(f32[32,2,32768]{2,1,0:T(2,128)} %reshape.243), calls=%async_computation.1 | async-start | bytes 16777216 | tf_op jit(solution)/shard_map/all_to_all | solution.py:106
  93.7 125.2 %all-reduce.4.cloned.1.call-start = ((), (), s32[]{:S(2)}) async-start(), calls=%async_computation.2 | async-start | bytes 1048576 | tf_op jit(solution)/shard_map/psum | solution.py:85
  105.7 4.8 %copy-start.1 = (f32[32,32768]{1,0:T(8,128)S(1)}, f32[32,32768]{1,0:T(8,128)}, u32[]{:S(2)}) copy-start(f32[32,32768]{1,0:T(8,128)} %get-tuple-element.392) | copy-start | bytes 12582916 | tf_op jit(solution)/shard_map/while
  117.1 2.0 copy-start.2
  119.2 6.1 %copy-start.11 = (s32[1,1,32,2]{2,3,1,0:T(2,128)S(1)}, s32[1,1,32,2]{2,3,1,0:T(2,128)}, u32[]{:S(2)}) copy-start(s32[1,1,32,2]{2,3,1,0:T(2,128)} %param.24) | copy-start | bytes 772
  125.3 139.9 %all-gather.4.cloned.1.call-start = ((), (), s32[]{:S(2)}) async-start(), calls=%async_computation.3 | async-start | bytes 2621440 | tf_op jit(solution)/shard_map/all_gather | solution.py:118
  211.8 7.3 %copy-start.3 = (bf16[512,256]{1,0:T(8,128)(2,1)S(1)}, bf16[512,256]{1,0:T(8,128)(2,1)}, u32[]{:S(2)}) copy-start(bf16[512,256]{1,0:T(8,128)(2,1)} %param.15) | copy-start | bytes 786436
  211.8 7.3 %copy-start.5 = (bf16[512,256]{1,0:T(8,128)(2,1)S(1)}, bf16[512,256]{1,0:T(8,128)(2,1)}, u32[]{:S(2)}) copy-start(bf16[512,256]{1,0:T(8,128)(2,1)} %param.25) | copy-start | bytes 786436
  218.9 180.5 %all-reduce.6.cloned.1.call-start = ((), (), s32[]{:S(2)}) async-start(), calls=%async_computation.4 | async-start | bytes 4718592 | tf_op jit(solution)/shard_map/psum | solution.py:86
  220.1 7.7 %copy-start.6 = (f32[4,128,256]{2,1,0:T(8,128)S(1)}, f32[4,128,256]{2,1,0:T(8,128)}, u32[]{:S(2)}) copy-start(f32[4,128,256]{2,1,0:T(8,128)} %all-reduce.4.cloned.1.call-done) | copy-start | bytes 1572868
  220.1 7.7 %copy-start.7 = (bf16[256,256]{1,0:T(8,128)(2,1)S(1)}, bf16[256,256]{1,0:T(8,128)(2,1)}, u32[]{:S(2)}) copy-start(bf16[256,256]{1,0:T(8,128)(2,1)} %param.17) | copy-start | bytes 393220
  399.4 3.1 copy-start.8
Sparse Core Ops, SparseCore 0:
  125.4 42.8 all-reduce.3
  219.0 46.1 all-gather.3
Sparse Core Ops, SparseCore 1:
  227.8 171.5 all-reduce.5
